TPU v7x, 128 devices: a whole 4x4x4 slice. The times are simulated.
128 devices in a mesh: req: 32 (over x, z, core), mlp: 4 (over y).
Axes of the slice: x: 4, y: 4, z: 4, core: 2. Of those that a mesh axis runs over, the one named last changes fastest.
Arguments:
- queries: bfloat16 [16896, 2048], P('req', 'mlp'), may hold values from -6 to 6
- key_cache: bfloat16 [2560, 128, 1024], P('req', None, 'mlp'), may hold values from -6 to 6
- value_cache: bfloat16 [2560, 128, 1024], P('req', None, 'mlp'), may hold values from -6 to 6
- decode_len: int32 [512], P('req'), may hold values from 1 to 4096, as said below
- stretch_start: int32 [32], P('req'), may hold values from 0 to 3584, as said below
- page_table: int32 [544, 32], P('req'), may hold values from 0 to 79, as said below
- hidden_in: bfloat16 [16896, 2304], P('req')
- o_weight: bfloat16 [2048, 2304], P('mlp'), may hold values from -0.125 to 0.125
- attn_gain: float32 [2304], replicated, may hold values from 0.1 to 1.9
- ffn_in_gain: float32 [2304], replicated, may hold values from 0.1 to 1.9
- ffn_out_gain: float32 [2304], replicated, may hold values from 0.1 to 1.9
- w_gate: bfloat16 [2304, 9216], P('req', 'mlp'), may hold values from -0.125 to 0.125
- w_up: bfloat16 [2304, 9216], P('req', 'mlp'), may hold values from -0.125 to 0.125
- w_down: bfloat16 [2304, 9216], P('req', 'mlp')
Outputs:
- layer_out: bfloat16 [16896, 2304], P('req', 'mlp')
Inputs may be any that keep to these rules, and one draw needn't show every extreme that they name: `decode_len`: each decode request's tokens fill its first pages; request 1 of req index 1 holds 4096 tokens. `stretch_start`: req index 0 starts at 3584, req index 1 at 0. `page_table`: row j of req index r's block of 17 rows names request j's pages by slot in that index's own pool of 80 pages; the slots holding a req index's tokens are all distinct; entries past a request's last page are valid slots that hold none of its tokens.
All inputs are finite; a program needn't handle non-finite values.
Results may differ from a plain program's by a relative error of at most 0.014.
Values may be sent and summed in bfloat16 or wider, within the bound.
A program may use at most 128 MiB of HBM per device.

v0:
```python
import math
import jax
import jax.numpy as jnp
from jax import lax
from jax.sharding import PartitionSpec as P

H = 8
KVH = 4
HD = 256
PRE_DEV = 512
DEC_DEV = 16
EPS = 1e-06
CAP = 50.0


def rms(values, gain):
    return values * lax.rsqrt(jnp.mean(values * values, axis=-1, keepdims=True) + EPS) * gain


def capped_weight(scores, visible):
    capped = CAP * jnp.tanh(scores / (16.0 * CAP))
    return jnp.where(visible, jnp.exp(capped), jnp.float32(0.0))


def attend(queries, key_cache, value_cache, decode_len, stretch_start, page_table):
    rows = queries.shape[0]
    local_kv = key_cache.shape[2] // HD
    rep = H // KVH
    page_len = key_cache.shape[1]
    max_pages = page_table.shape[1]
    requests = page_table.shape[0]
    block = math.gcd(max_pages, max(1, 512 // page_len))
    span = block * page_len
    query = queries.reshape(rows, local_kv, rep, HD)
    pre_q = query[:PRE_DEV]
    dec_q = query[PRE_DEV:]
    start = stretch_start[0]
    limit = start + jnp.arange(PRE_DEV, dtype=jnp.int32) + 1
    need = jnp.maximum(
        (start + PRE_DEV + page_len - 1) // page_len,
        jnp.max((decode_len + page_len - 1) // page_len),
    )
    blocks = (need + block - 1) // block

    def step(index, carry):
        pre_num, pre_den, dec_num, dec_den = carry
        slots = lax.dynamic_slice_in_dim(page_table, index * block, block, 1)
        keys = key_cache[slots].reshape(requests, span, local_kv, HD)
        vals = value_cache[slots].reshape(requests, span, local_kv, HD)
        position = index * span + jnp.arange(span, dtype=jnp.int32)
        pre_scores = jnp.einsum(
            "rghd,tgd->rght", pre_q, keys[0], preferred_element_type=jnp.float32
        )
        pre_weight = capped_weight(
            pre_scores, position[None, None, None, :] < limit[:, None, None, None]
        )
        pre_num = pre_num + jnp.einsum(
            "rght,tgd->rghd",
            pre_weight.astype(jnp.bfloat16),
            vals[0],
            preferred_element_type=jnp.float32,
        )
        pre_den = pre_den + jnp.sum(pre_weight, axis=-1)
        dec_scores = jnp.einsum(
            "rghd,rtgd->rght", dec_q, keys[1:], preferred_element_type=jnp.float32
        )
        dec_weight = capped_weight(
            dec_scores, position[None, None, None, :] < decode_len[:, None, None, None]
        )
        dec_num = dec_num + jnp.einsum(
            "rght,rtgd->rghd",
            dec_weight.astype(jnp.bfloat16),
            vals[1:],
            preferred_element_type=jnp.float32,
        )
        dec_den = dec_den + jnp.sum(dec_weight, axis=-1)
        return (pre_num, pre_den, dec_num, dec_den)

    start_carry = (
        jnp.zeros((PRE_DEV, local_kv, rep, HD), jnp.float32),
        jnp.zeros((PRE_DEV, local_kv, rep), jnp.float32),
        jnp.zeros((DEC_DEV, local_kv, rep, HD), jnp.float32),
        jnp.zeros((DEC_DEV, local_kv, rep), jnp.float32),
    )
    pre_num, pre_den, dec_num, dec_den = lax.fori_loop(0, blocks, step, start_carry)
    pre_out = (pre_num / pre_den[..., None]).astype(jnp.bfloat16)
    dec_out = (dec_num / dec_den[..., None]).astype(jnp.bfloat16)
    return jnp.concatenate([pre_out, dec_out], axis=0).reshape(rows, local_kv * rep * HD)


def per_device(
    queries,
    key_cache,
    value_cache,
    decode_len,
    stretch_start,
    page_table,
    hidden_in,
    o_weight,
    attn_gain,
    ffn_in_gain,
    ffn_out_gain,
    w_gate,
    w_up,
    w_down,
):
    attended = attend(queries, key_cache, value_cache, decode_len, stretch_start, page_table)
    projected = lax.psum(
        jnp.dot(attended, o_weight, preferred_element_type=jnp.float32).astype(jnp.bfloat16), "mlp"
    ).astype(jnp.float32)
    resid = hidden_in.astype(jnp.float32) + rms(projected, attn_gain)
    normed = rms(resid, ffn_in_gain).astype(jnp.bfloat16)
    gate = jnp.dot(
        normed,
        lax.all_gather(w_gate, "req", axis=0, tiled=True),
        preferred_element_type=jnp.float32,
    )
    up_part = jnp.dot(
        normed, lax.all_gather(w_up, "req", axis=0, tiled=True), preferred_element_type=jnp.float32
    )
    act = (jax.nn.gelu(gate, approximate=True) * up_part).astype(jnp.bfloat16)
    partial_out = lax.dot_general(
        act,
        lax.all_gather(w_down, "req", axis=0, tiled=True),
        (((1,), (1,)), ((), ())),
        preferred_element_type=jnp.float32,
    )
    width = hidden_in.shape[1] // lax.axis_size("mlp")
    first = lax.axis_index("mlp") * width
    total = lax.psum(partial_out.astype(jnp.bfloat16), "mlp").astype(jnp.float32)
    combined = resid + rms(total, ffn_out_gain)
    result = lax.dynamic_slice_in_dim(combined, first, width, 1)
    return result.astype(jnp.bfloat16)


def solution(mesh):
    return jax.shard_map(
        per_device,
        mesh=mesh,
        in_specs=(
            P("req", "mlp"),
            P("req", None, "mlp"),
            P("req", None, "mlp"),
            P("req"),
            P("req"),
            P("req", None),
            P("req", None),
            P("mlp", None),
            P(),
            P(),
            P(),
            P("req", "mlp"),
            P("req", "mlp"),
            P("req", "mlp"),
        ),
        out_specs=P("req", "mlp"),
        check_vma=False,
    )
```

profile of v0, /device:TPU:1, one launch (start us, length us, event | category | flops | bytes accessed | tf_op | source)
XLA Modules:
  0.0 542.8 jit_solution(7240394064184673819)
XLA Ops:
  13.4 251.5 %while.17 = (s32[]{:T(128)}, f32[512,1,2,256]{0,3,2,1:T(8,128)S(1)}, f32[512,1,2]{0,2,1:T(2,128)S(1)}, f32[16,1,2,256]{3,2,0,1:T(2,128)S(1)}, f32[16,1,2]{0,2,1:...) while((s32[]{:T(128)}, ...), condition=%wide.region_4.5_spmd.clone, body=%wide.region_1.4_spmd.clone.sunk | while | flops 556894976 | bytes 58393828 | solution.py:85
  14.3 7.9 %gather_fusion.1 = bf16[68,128,256]{2,1,0:T(8,128)(2,1)} fusion(bf16[80,128,256]{2,1,0:T(8,128)(2,1)} %get-tuple-element.310, s32[1024]{0:T(1024)S(1)} %pad_clamp_fusion.2), kind=kCustom, calls=%fused_computation.1.clone.clone.1 | custom fusion | bytes 8913168 | tf_op jit(solution)/shard_map/while/body/gather | solution.py:48
  27.7 7.9 %gather_fusion = bf16[68,128,256]{2,1,0:T(8,128)(2,1)} fusion(bf16[80,128,256]{2,1,0:T(8,128)(2,1)} %get-tuple-element.309, s32[1024]{0:T(1024)S(1)} %pad_clamp_fusion.2), kind=kCustom, calls=%fused_computation.clone.clone.1 | custom fusion | bytes 8913168 | tf_op jit(solution)/shard_map/while/body/gather | solution.py:49
  45.7 7.9 %gather_fusion.1 = bf16[68,128,256]{2,1,0:T(8,128)(2,1)} fusion(bf16[80,128,256]{2,1,0:T(8,128)(2,1)} %get-tuple-element.310, s32[1024]{0:T(1024)S(1)} %pad_clamp_fusion.2), kind=kCustom, calls=%fused_computation.1.clone.clone.1 | custom fusion | bytes 8913168 | tf_op jit(solution)/shard_map/while/body/gather | solution.py:48
  59.2 7.9 %gather_fusion = bf16[68,128,256]{2,1,0:T(8,128)(2,1)} fusion(bf16[80,128,256]{2,1,0:T(8,128)(2,1)} %get-tuple-element.309, s32[1024]{0:T(1024)S(1)} %pad_clamp_fusion.2), kind=kCustom, calls=%fused_computation.clone.clone.1 | custom fusion | bytes 8913168 | tf_op jit(solution)/shard_map/while/body/gather | solution.py:49
  77.1 7.9 %gather_fusion.1 = bf16[68,128,256]{2,1,0:T(8,128)(2,1)} fusion(bf16[80,128,256]{2,1,0:T(8,128)(2,1)} %get-tuple-element.310, s32[1024]{0:T(1024)S(1)} %pad_clamp_fusion.2), kind=kCustom, calls=%fused_computation.1.clone.clone.1 | custom fusion | bytes 8913168 | tf_op jit(solution)/shard_map/while/body/gather | solution.py:48
  90.6 7.9 %gather_fusion = bf16[68,128,256]{2,1,0:T(8,128)(2,1)} fusion(bf16[80,128,256]{2,1,0:T(8,128)(2,1)} %get-tuple-element.309, s32[1024]{0:T(1024)S(1)} %pad_clamp_fusion.2), kind=kCustom, calls=%fused_computation.clone.clone.1 | custom fusion | bytes 8913168 | tf_op jit(solution)/shard_map/while/body/gather | solution.py:49
  108.6 7.9 %gather_fusion.1 = bf16[68,128,256]{2,1,0:T(8,128)(2,1)} fusion(bf16[80,128,256]{2,1,0:T(8,128)(2,1)} %get-tuple-element.310, s32[1024]{0:T(1024)S(1)} %pad_clamp_fusion.2), kind=kCustom, calls=%fused_computation.1.clone.clone.1 | custom fusion | bytes 8913168 | tf_op jit(solution)/shard_map/while/body/gather | solution.py:48
  122.0 7.9 %gather_fusion = bf16[68,128,256]{2,1,0:T(8,128)(2,1)} fusion(bf16[80,128,256]{2,1,0:T(8,128)(2,1)} %get-tuple-element.309, s32[1024]{0:T(1024)S(1)} %pad_clamp_fusion.2), kind=kCustom, calls=%fused_computation.clone.clone.1 | custom fusion | bytes 8913168 | tf_op jit(solution)/shard_map/while/body/gather | solution.py:49
  140.0 7.9 %gather_fusion.1 = bf16[68,128,256]{2,1,0:T(8,128)(2,1)} fusion(bf16[80,128,256]{2,1,0:T(8,128)(2,1)} %get-tuple-element.310, s32[1024]{0:T(1024)S(1)} %pad_clamp_fusion.2), kind=kCustom, calls=%fused_computation.1.clone.clone.1 | custom fusion | bytes 8913168 | tf_op jit(solution)/shard_map/while/body/gather | solution.py:48
  153.5 7.9 %gather_fusion = bf16[68,128,256]{2,1,0:T(8,128)(2,1)} fusion(bf16[80,128,256]{2,1,0:T(8,128)(2,1)} %get-tuple-element.309, s32[1024]{0:T(1024)S(1)} %pad_clamp_fusion.2), kind=kCustom, calls=%fused_computation.clone.clone.1 | custom fusion | bytes 8913168 | tf_op jit(solution)/shard_map/while/body/gather | solution.py:49
  171.4 7.9 %gather_fusion.1 = bf16[68,128,256]{2,1,0:T(8,128)(2,1)} fusion(bf16[80,128,256]{2,1,0:T(8,128)(2,1)} %get-tuple-element.310, s32[1024]{0:T(1024)S(1)} %pad_clamp_fusion.2), kind=kCustom, calls=%fused_computation.1.clone.clone.1 | custom fusion | bytes 8913168 | tf_op jit(solution)/shard_map/while/body/gather | solution.py:48
  184.9 7.9 %gather_fusion = bf16[68,128,256]{2,1,0:T(8,128)(2,1)} fusion(bf16[80,128,256]{2,1,0:T(8,128)(2,1)} %get-tuple-element.309, s32[1024]{0:T(1024)S(1)} %pad_clamp_fusion.2), kind=kCustom, calls=%fused_computation.clone.clone.1 | custom fusion | bytes 8913168 | tf_op jit(solution)/shard_map/while/body/gather | solution.py:49
  202.9 7.9 %gather_fusion.1 = bf16[68,128,256]{2,1,0:T(8,128)(2,1)} fusion(bf16[80,128,256]{2,1,0:T(8,128)(2,1)} %get-tuple-element.310, s32[1024]{0:T(1024)S(1)} %pad_clamp_fusion.2), kind=kCustom, calls=%fused_computation.1.clone.clone.1 | custom fusion | bytes 8913168 | tf_op jit(solution)/shard_map/while/body/gather | solution.py:48
  216.4 7.9 %gather_fusion = bf16[68,128,256]{2,1,0:T(8,128)(2,1)} fusion(bf16[80,128,256]{2,1,0:T(8,128)(2,1)} %get-tuple-element.309, s32[1024]{0:T(1024)S(1)} %pad_clamp_fusion.2), kind=kCustom, calls=%fused_computation.clone.clone.1 | custom fusion | bytes 8913168 | tf_op jit(solution)/shard_map/while/body/gather | solution.py:49
  234.3 7.9 %gather_fusion.1 = bf16[68,128,256]{2,1,0:T(8,128)(2,1)} fusion(bf16[80,128,256]{2,1,0:T(8,128)(2,1)} %get-tuple-element.310, s32[1024]{0:T(1024)S(1)} %pad_clamp_fusion.2), kind=kCustom, calls=%fused_computation.1.clone.clone.1 | custom fusion | bytes 8913168 | tf_op jit(solution)/shard_map/while/body/gather | solution.py:48
  247.8 7.9 %gather_fusion = bf16[68,128,256]{2,1,0:T(8,128)(2,1)} fusion(bf16[80,128,256]{2,1,0:T(8,128)(2,1)} %get-tuple-element.309, s32[1024]{0:T(1024)S(1)} %pad_clamp_fusion.2), kind=kCustom, calls=%fused_computation.clone.clone.1 | custom fusion | bytes 8913168 | tf_op jit(solution)/shard_map/while/body/gather | solution.py:49
  271.6 64.7 %all-reduce.3.cloned.1.call-done = bf16[528,2304]{1,0:T(8,128)(2,1)} async-done(((bf16[528,2304]{1,0:T(8,128)(2,1)}), bf16[528,2304]{1,0:T(8,128)(2,1)}) %all-reduce.3.cloned.1.call-update) | async-done | bytes 2433040 | tf_op jit(solution)/shard_map/psum | solution.py:108
  344.4 12.5 %fusion.28 = f32[528,2304]{1,0:T(8,128)} fusion(bf16[2304,2304]{1,0:T(8,128)(2,1)} %all-gather.4.cloned.1.call-done, f32[528,2304]{1,0:T(8,128)} %get-tuple-element.163, f32[2304]{0:T(1024)S(1)} %copy-done.4, f32[528]{0:T(1024)S(1)} %add_rsqrt_fusion.1), kind=kOutput, calls=%fused_computation.62 | convolution fusion | flops 5609336832 | bytes 20360256 | tf_op jit(solution)/shard_map/dot_general | solution.py:113
  356.9 36.1 %all-gather.6.cloned.1.call-done = bf16[2304,2304]{1,0:T(8,128)(2,1)} async-done(((bf16[72,2304]{1,0:T(8,128)(2,1)}), bf16[2304,2304]{1,0:T(8,128)(2,1)}) %all-gather.6.cloned.1.call-update) | async-done | bytes 10616848 | tf_op jit(solution)/shard_map/all_gather | solution.py:119
  393.0 12.9 %fusion.24 = bf16[528,2304]{1,0:T(8,128)(2,1)} fusion(bf16[2304,2304]{1,0:T(8,128)(2,1)} %all-gather.6.cloned.1.call-done, f32[528,2304]{1,0:T(8,128)} %fusion.28, f32[528,2304]{1,0:T(8,128)} %get-tuple-element.163, f32[2304]{0:T(1024)S(1)} %copy-done.4, f32[528]{0:T(1024)S(1)} %add_rsqrt_fusion.1), kind=kOutput, calls=%fused_computation.44 | convolution fusion | flops 5621501952 | bytes 22793280 | tf_op jit(solution)/shard_map/dot_general | solution.py:118
  405.8 46.8 %all-gather.8.cloned.1.call-done = bf16[2304,2304]{1,0:T(8,128)(2,1)} async-done(((bf16[72,2304]{1,0:T(8,128)(2,1)}), bf16[2304,2304]{1,0:T(8,128)(2,1)}) %all-gather.8.cloned.1.call-update) | async-done | bytes 10616848 | tf_op jit(solution)/shard_map/all_gather | solution.py:124
  452.7 11.6 %convolution_convert_fusion = bf16[528,2304]{1,0:T(8,128)(2,1)} fusion(bf16[528,2304]{1,0:T(8,128)(2,1)} %fusion.24, bf16[2304,2304]{1,0:T(8,128)(2,1)} %all-gather.8.cloned.1.call-done), kind=kOutput, calls=%fused_computation.45 | convolution fusion | flops 5606903808 | bytes 15482880 | tf_op jit(solution)/shard_map/dot_general | solution.py:122
  465.1 62.5 %all-reduce.5.cloned.1.call-done = bf16[528,2304]{1,0:T(8,128)(2,1)} async-done(((bf16[528,2304]{1,0:T(8,128)(2,1)}), bf16[528,2304]{1,0:T(8,128)(2,1)}) %all-reduce.5.cloned.1.call-update) | async-done | bytes 2433040 | tf_op jit(solution)/shard_map/psum | solution.py:130
  (212 shorter events, 152.1 us)
Async XLA Ops:
  7.4 259.3 %copy-start = (bf16[512,2304]{1,0:T(8,128)(2,1)S(1)}, bf16[512,2304]{1,0:T(8,128)(2,1)}, u32[]{:S(2)}) copy-start(bf16[512,2304]{1,0:T(8,128)(2,1)} %param.23) | copy-start | bytes 7077892
  7.4 329.0 %all-reduce.3.cloned.1.call-start = ((), (), s32[]{:S(2)}) async-start(), calls=%async_computation | async-start | bytes 4866048 | tf_op jit(solution)/shard_map/psum | solution.py:108
  38.4 2.2 slice-start
  41.8 2.2 slice-start.1
  69.8 2.2 slice-start
  73.3 2.2 slice-start.1
  101.2 2.2 slice-start
  104.7 2.2 slice-start.1
  132.7 2.2 slice-start
  136.2 2.2 slice-start.1
  164.1 2.2 slice-start
  167.6 2.2 slice-start.1
  195.5 2.2 slice-start
  199.0 2.2 slice-start.1
  230.5 2.2 slice-start.1
  258.4 2.2 slice-start
  261.9 2.2 slice-start.1
  269.6 69.0 %copy-start.3 = (f32[2304]{0:T(1024)S(1)}, f32[2304]{0:T(1024)}, u32[]{:S(2)}) copy-start(f32[2304]{0:T(1024)} %param.24) | copy-start | bytes 27652
  269.6 74.8 %all-gather.4.cloned.1.call-start = ((), (), s32[]{:S(2)}) async-start(), calls=%async_computation.1 | async-start | bytes 10948608 | tf_op jit(solution)/shard_map/all_gather | solution.py:115
  270.2 122.7 %all-gather.6.cloned.1.call-start = ((), (), s32[]{:S(2)}) async-start(), calls=%async_computation.2 | async-start | bytes 10948608 | tf_op jit(solution)/shard_map/all_gather | solution.py:119
  270.8 181.9 %all-gather.8.cloned.1.call-start = ((), (), s32[]{:S(2)}) async-start(), calls=%async_computation.3 | async-start | bytes 10948608 | tf_op jit(solution)/shard_map/all_gather | solution.py:124
  271.4 256.2 %all-reduce.5.cloned.1.call-start = ((), (), s32[]{:S(2)}) async-start(), calls=%async_computation.4 | async-start | bytes 4866048 | tf_op jit(solution)/shard_map/psum | solution.py:130
  338.6 5.8 %copy-start.4 = (f32[2304]{0:T(1024)S(1)}, f32[2304]{0:T(1024)}, u32[]{:S(2)}) copy-start(f32[2304]{0:T(1024)} %param.25) | copy-start | bytes 27652
  529.8 5.4 copy-start.1
  (9 other events, 7.5 us)
Sparse Core Ops, SparseCore 0:
  269.8 66.5 all-reduce.2
  464.4 63.1 all-reduce.4
Sparse Core Ops, SparseCore 1:
  272.5 60.8 all-gather.3
  335.5 57.4 all-gather.5
  395.2 57.4 all-gather.7
where the time goes:
time: 546 us; the launch traced here: 543 us
  waiting for transfers between devices  212 us (39%)
  local copies, waits for them, and re-layouts  188 us (34%)
  matrix products  93.3 us (17%)
  other arithmetic  31.8 us (6%)
  between operations  16.6 us (3%)
    psum x1, waiting for transfers between devices, per_device(): lax.psum(jnp.dot(attended, o_weight, preferred_element_type=jnp.float32)....  64.7 us
    gather x8, local copies, waits for them, and re-layouts, step(): vals = value_cache[slots].reshape(requests, span, local_kv, HD)  63.5 us
    gather x8, local copies, waits for them, and re-layouts, step(): keys = key_cache[slots].reshape(requests, span, local_kv, HD)  62.9 us
    psum x1, waiting for transfers between devices, per_device(): lax.psum(partial_out.astype(jnp.bfloat16), 'mlp').astype(jnp.float32)  62.5 us
    all_gather x1, waiting for transfers between devices, per_device(): lax.all_gather(w_down, 'req', axis=0, tiled=True)  46.8 us
    all_gather x1, waiting for transfers between devices, per_device(): lax.all_gather(w_up, 'req', axis=0, tiled=True)  36.1 us
    dot_general x8, matrix products, step(): jnp.einsum('rghd,tgd->rght', pre_q, keys[0], preferred_element_type=jnp.f...  24.4 us
    slice x16, local copies, waits for them, and re-layouts, step(): vals[1:]  17.6 us
  transfers between devices with their start and end apart: 5, of which 4 were waited for; matrix products, arithmetic and copies ran while one was open for 6% of the time, Pallas kernels for 0%

commit v1 on v0

--- a/solution.py
+++ b/solution.py
@@ -119,11 +119,14 @@
         normed, lax.all_gather(w_up, "req", axis=0, tiled=True), preferred_element_type=jnp.float32
     )
     act = (jax.nn.gelu(gate, approximate=True) * up_part).astype(jnp.bfloat16)
+
+    def return_all_patch(unit):
+        y = jnp.stack([unit for _ in range(lax.axis_size("req"))], 0)
+        tile_out = lax.all_to_all(y, "req", 0, 0)
+        return jnp.concatenate(tile_out, 0)
+
     partial_out = lax.dot_general(
-        act,
-        lax.all_gather(w_down, "req", axis=0, tiled=True),
-        (((1,), (1,)), ((), ())),
-        preferred_element_type=jnp.float32,
+        act, return_all_patch(w_down), (((1,), (1,)), ((), ())), preferred_element_type=jnp.float32
     )
     width = hidden_in.shape[1] // lax.axis_size("mlp")
     first = lax.axis_index("mlp") * width

time: 546 us -> 606 us (1.11)
  waiting for transfers between devices: 212 us -> 259 us
  starting transfers between devices: 0.35 us -> 9.11 us
    all_gather x1, waiting for transfers between devices: 0.01 us -> 88.9 us  [per_device(): lax.all_gather(w_gate, 'req', axis=0, tiled=True)]
    all_gather x1 -> x0, waiting for transfers between devices: 46.8 us -> none  [per_device(): lax.all_gather(w_down, 'req', axis=0, tiled=True)]
    all_gather x1, waiting for transfers between devices: 36.1 us -> 54.7 us  [per_device(): lax.all_gather(w_up, 'req', axis=0, tiled=True)]
    psum x1, waiting for transfers between devices: 64.7 us -> 51.9 us  [per_device(): lax.psum(jnp.dot(attended, o_weight, preferred_element_type=jnp.float32)....]
    all_to_all x0 -> x1, starting transfers between devices: none -> 8.8 us  [return_all_patch(): tile_out = lax.all_to_all(y, 'req', 0, 0)]
where the time goes in v1:
time: 606 us; the launch traced here: 603 us
  waiting for transfers between devices  259 us (43%)
  local copies, waits for them, and re-layouts  193 us (32%)
  matrix products  93.1 us (15%)
  other arithmetic  31.9 us (5%)
  between operations  16.5 us (3%)
  starting transfers between devices  9.11 us (2%)
    all_gather x1, waiting for transfers between devices, per_device(): lax.all_gather(w_gate, 'req', axis=0, tiled=True)  88.9 us
    gather x8, local copies, waits for them, and re-layouts, step(): vals = value_cache[slots].reshape(requests, span, local_kv, HD)  63.5 us
    gather x8, local copies, waits for them, and re-layouts, step(): keys = key_cache[slots].reshape(requests, span, local_kv, HD)  62.9 us
    psum x1, waiting for transfers between devices, per_device(): lax.psum(partial_out.astype(jnp.bfloat16), 'mlp').astype(jnp.float32)  62.5 us
    all_gather x1, waiting for transfers between devices, per_device(): lax.all_gather(w_up, 'req', axis=0, tiled=True)  54.7 us
    psum x1, waiting for transfers between devices, per_device(): lax.psum(jnp.dot(attended, o_weight, preferred_element_type=jnp.float32)....  51.9 us
    dot_general x8, matrix products, step(): jnp.einsum('rghd,tgd->rght', pre_q, keys[0], preferred_element_type=jnp.f...  24.4 us
    slice x16, local copies, waits for them, and re-layouts, step(): vals[1:]  17.6 us
  transfers between devices with their start and end apart: 5, of which 4 were waited for; matrix products, arithmetic and copies ran while one was open for 6% of the time, Pallas kernels for 0%

profile of v1, /device:TPU:1, one launch (start us, length us, event | category | flops | bytes accessed | tf_op | source)
XLA Modules:
  0.0 603.3 jit_solution(13582177318966095978)
XLA Ops:
  13.4 251.5 %while.17 = (s32[]{:T(128)}, f32[512,1,2,256]{0,3,2,1:T(8,128)S(1)}, f32[512,1,2]{0,2,1:T(2,128)S(1)}, f32[16,1,2,256]{3,2,0,1:T(2,128)S(1)}, f32[16,1,2]{0,2,1:...) while((s32[]{:T(128)}, ...), condition=%wide.region_4.5_spmd.clone, body=%wide.region_1.4_spmd.clone.sunk | while | flops 556894976 | bytes 58393828 | solution.py:85
  27.7 7.9 %gather_fusion = bf16[68,128,256]{2,1,0:T(8,128)(2,1)} fusion(bf16[80,128,256]{2,1,0:T(8,128)(2,1)} %get-tuple-element.309, s32[1024]{0:T(1024)S(1)} %pad_clamp_fusion.2), kind=kCustom, calls=%fused_computation.clone.clone.1 | custom fusion | bytes 8913168 | tf_op jit(solution)/shard_map/while/body/gather | solution.py:49
  45.7 7.9 %gather_fusion.1 = bf16[68,128,256]{2,1,0:T(8,128)(2,1)} fusion(bf16[80,128,256]{2,1,0:T(8,128)(2,1)} %get-tuple-element.310, s32[1024]{0:T(1024)S(1)} %pad_clamp_fusion.2), kind=kCustom, calls=%fused_computation.1.clone.clone.1 | custom fusion | bytes 8913168 | tf_op jit(solution)/shard_map/while/body/gather | solution.py:48
  59.2 7.9 %gather_fusion = bf16[68,128,256]{2,1,0:T(8,128)(2,1)} fusion(bf16[80,128,256]{2,1,0:T(8,128)(2,1)} %get-tuple-element.309, s32[1024]{0:T(1024)S(1)} %pad_clamp_fusion.2), kind=kCustom, calls=%fused_computation.clone.clone.1 | custom fusion | bytes 8913168 | tf_op jit(solution)/shard_map/while/body/gather | solution.py:49
  77.1 7.9 %gather_fusion.1 = bf16[68,128,256]{2,1,0:T(8,128)(2,1)} fusion(bf16[80,128,256]{2,1,0:T(8,128)(2,1)} %get-tuple-element.310, s32[1024]{0:T(1024)S(1)} %pad_clamp_fusion.2), kind=kCustom, calls=%fused_computation.1.clone.clone.1 | custom fusion | bytes 8913168 | tf_op jit(solution)/shard_map/while/body/gather | solution.py:48
  90.6 7.9 %gather_fusion = bf16[68,128,256]{2,1,0:T(8,128)(2,1)} fusion(bf16[80,128,256]{2,1,0:T(8,128)(2,1)} %get-tuple-element.309, s32[1024]{0:T(1024)S(1)} %pad_clamp_fusion.2), kind=kCustom, calls=%fused_computation.clone.clone.1 | custom fusion | bytes 8913168 | tf_op jit(solution)/shard_map/while/body/gather | solution.py:49
  108.6 7.9 %gather_fusion.1 = bf16[68,128,256]{2,1,0:T(8,128)(2,1)} fusion(bf16[80,128,256]{2,1,0:T(8,128)(2,1)} %get-tuple-element.310, s32[1024]{0:T(1024)S(1)} %pad_clamp_fusion.2), kind=kCustom, calls=%fused_computation.1.clone.clone.1 | custom fusion | bytes 8913168 | tf_op jit(solution)/shard_map/while/body/gather | solution.py:48
  122.0 7.9 %gather_fusion = bf16[68,128,256]{2,1,0:T(8,128)(2,1)} fusion(bf16[80,128,256]{2,1,0:T(8,128)(2,1)} %get-tuple-element.309, s32[1024]{0:T(1024)S(1)} %pad_clamp_fusion.2), kind=kCustom, calls=%fused_computation.clone.clone.1 | custom fusion | bytes 8913168 | tf_op jit(solution)/shard_map/while/body/gather | solution.py:49
  140.0 7.9 %gather_fusion.1 = bf16[68,128,256]{2,1,0:T(8,128)(2,1)} fusion(bf16[80,128,256]{2,1,0:T(8,128)(2,1)} %get-tuple-element.310, s32[1024]{0:T(1024)S(1)} %pad_clamp_fusion.2), kind=kCustom, calls=%fused_computation.1.clone.clone.1 | custom fusion | bytes 8913168 | tf_op jit(solution)/shard_map/while/body/gather | solution.py:48
  153.5 7.9 %gather_fusion = bf16[68,128,256]{2,1,0:T(8,128)(2,1)} fusion(bf16[80,128,256]{2,1,0:T(8,128)(2,1)} %get-tuple-element.309, s32[1024]{0:T(1024)S(1)} %pad_clamp_fusion.2), kind=kCustom, calls=%fused_computation.clone.clone.1 | custom fusion | bytes 8913168 | tf_op jit(solution)/shard_map/while/body/gather | solution.py:49
  171.4 7.9 %gather_fusion.1 = bf16[68,128,256]{2,1,0:T(8,128)(2,1)} fusion(bf16[80,128,256]{2,1,0:T(8,128)(2,1)} %get-tuple-element.310, s32[1024]{0:T(1024)S(1)} %pad_clamp_fusion.2), kind=kCustom, calls=%fused_computation.1.clone.clone.1 | custom fusion | bytes 8913168 | tf_op jit(solution)/shard_map/while/body/gather | solution.py:48
  184.9 7.9 %gather_fusion = bf16[68,128,256]{2,1,0:T(8,128)(2,1)} fusion(bf16[80,128,256]{2,1,0:T(8,128)(2,1)} %get-tuple-element.309, s32[1024]{0:T(1024)S(1)} %pad_clamp_fusion.2), kind=kCustom, calls=%fused_computation.clone.clone.1 | custom fusion | bytes 8913168 | tf_op jit(solution)/shard_map/while/body/gather | solution.py:49
  202.9 7.9 %gather_fusion.1 = bf16[68,128,256]{2,1,0:T(8,128)(2,1)} fusion(bf16[80,128,256]{2,1,0:T(8,128)(2,1)} %get-tuple-element.310, s32[1024]{0:T(1024)S(1)} %pad_clamp_fusion.2), kind=kCustom, calls=%fused_computation.1.clone.clone.1 | custom fusion | bytes 8913168 | tf_op jit(solution)/shard_map/while/body/gather | solution.py:48
  216.4 7.9 %gather_fusion = bf16[68,128,256]{2,1,0:T(8,128)(2,1)} fusion(bf16[80,128,256]{2,1,0:T(8,128)(2,1)} %get-tuple-element.309, s32[1024]{0:T(1024)S(1)} %pad_clamp_fusion.2), kind=kCustom, calls=%fused_computation.clone.clone.1 | custom fusion | bytes 8913168 | tf_op jit(solution)/shard_map/while/body/gather | solution.py:49
  234.3 7.9 %gather_fusion.1 = bf16[68,128,256]{2,1,0:T(8,128)(2,1)} fusion(bf16[80,128,256]{2,1,0:T(8,128)(2,1)} %get-tuple-element.310, s32[1024]{0:T(1024)S(1)} %pad_clamp_fusion.2), kind=kCustom, calls=%fused_computation.1.clone.clone.1 | custom fusion | bytes 8913168 | tf_op jit(solution)/shard_map/while/body/gather | solution.py:48
  247.8 7.9 %gather_fusion = bf16[68,128,256]{2,1,0:T(8,128)(2,1)} fusion(bf16[80,128,256]{2,1,0:T(8,128)(2,1)} %get-tuple-element.309, s32[1024]{0:T(1024)S(1)} %pad_clamp_fusion.2), kind=kCustom, calls=%fused_computation.clone.clone.1 | custom fusion | bytes 8913168 | tf_op jit(solution)/shard_map/while/body/gather | solution.py:49
  275.4 8.8 %all-to-all-start = ((bf16[32,72,2304]{2,1,0:T(8,128)(2,1)}), bf16[32,72,2304]{2,1,0:T(8,128)(2,1)}, u32[]{:S(2)}, u32[]{:S(2)}) async-start(bf16[32,72,2304]{2,1,0:T(8,128)(2,1)} %stack.2), calls=%async_computation | async-start | bytes 21233664 | tf_op jit(solution)/shard_map/all_to_all | solution.py:125
  284.5 51.9 %all-reduce.3.cloned.1.call-done = bf16[528,2304]{1,0:T(8,128)(2,1)} async-done(((bf16[528,2304]{1,0:T(8,128)(2,1)}), bf16[528,2304]{1,0:T(8,128)(2,1)}) %all-reduce.3.cloned.1.call-update) | async-done | bytes 2433040 | tf_op jit(solution)/shard_map/psum | solution.py:108
  344.5 88.9 %all-gather.3.cloned.1.call-done = bf16[2304,2304]{1,0:T(8,128)(2,1)} async-done(((bf16[72,2304]{1,0:T(8,128)(2,1)}), bf16[2304,2304]{1,0:T(8,128)(2,1)}) %all-gather.3.cloned.1.call-update) | async-done | bytes 10616848 | tf_op jit(solution)/shard_map/all_gather | solution.py:115
  433.4 12.3 %fusion.28 = f32[528,2304]{1,0:T(8,128)} fusion(bf16[2304,2304]{1,0:T(8,128)(2,1)} %all-gather.3.cloned.1.call-done, f32[528,2304]{1,0:T(8,128)} %get-tuple-element.163, f32[2304]{0:T(1024)S(1)} %copy-done.5, f32[528]{0:T(1024)S(1)} %add_rsqrt_fusion.1), kind=kOutput, calls=%fused_computation.62 | convolution fusion | flops 5609336832 | bytes 20360256 | tf_op jit(solution)/shard_map/dot_general | solution.py:113
  445.7 54.7 %all-gather.5.cloned.1.call-done = bf16[2304,2304]{1,0:T(8,128)(2,1)} async-done(((bf16[72,2304]{1,0:T(8,128)(2,1)}), bf16[2304,2304]{1,0:T(8,128)(2,1)}) %all-gather.5.cloned.1.call-update) | async-done | bytes 10616848 | tf_op jit(solution)/shard_map/all_gather | solution.py:119
  500.5 12.9 %fusion.24 = bf16[528,2304]{1,0:T(8,128)(2,1)} fusion(bf16[2304,2304]{1,0:T(8,128)(2,1)} %all-gather.5.cloned.1.call-done, f32[528,2304]{1,0:T(8,128)} %fusion.28, f32[528,2304]{1,0:T(8,128)} %get-tuple-element.163, f32[2304]{0:T(1024)S(1)} %copy-done.5, f32[528]{0:T(1024)S(1)} %add_rsqrt_fusion.1), kind=kOutput, calls=%fused_computation.44 | convolution fusion | flops 5621501952 | bytes 22793280 | tf_op jit(solution)/shard_map/dot_general | solution.py:118
  513.4 11.5 %convolution_convert_fusion = bf16[528,2304]{1,0:T(8,128)(2,1)} fusion(bf16[528,2304]{1,0:T(8,128)(2,1)} %fusion.24, bf16[2304,2304]{1,0:T(8,128)(2,1)} %bitcast.5), kind=kOutput, calls=%fused_computation.45 | convolution fusion | flops 5606903808 | bytes 15482880 | tf_op jit(solution)/shard_map/dot_general | solution.py:128
  525.7 62.5 %all-reduce.5.cloned.1.call-done = bf16[528,2304]{1,0:T(8,128)(2,1)} async-done(((bf16[528,2304]{1,0:T(8,128)(2,1)}), bf16[528,2304]{1,0:T(8,128)(2,1)}) %all-reduce.5.cloned.1.call-update) | async-done | bytes 2433040 | tf_op jit(solution)/shard_map/psum | solution.py:133
  (214 shorter events, 164.1 us)
Async XLA Ops:
  7.4 259.3 %copy-start = (bf16[512,2304]{1,0:T(8,128)(2,1)S(1)}, bf16[512,2304]{1,0:T(8,128)(2,1)}, u32[]{:S(2)}) copy-start(bf16[512,2304]{1,0:T(8,128)(2,1)} %param.23) | copy-start | bytes 7077892
  7.4 329.0 %all-reduce.3.cloned.1.call-start = ((), (), s32[]{:S(2)}) async-start(), calls=%async_computation.1 | async-start | bytes 4866048 | tf_op jit(solution)/shard_map/psum | solution.py:108
  38.4 2.2 slice-start
  41.8 2.2 slice-start.1
  69.8 2.2 slice-start
  73.3 2.2 slice-start.1
  101.2 2.2 slice-start
  104.7 2.2 slice-start.1
  132.7 2.2 slice-start
  136.2 2.2 slice-start.1
  167.6 2.2 slice-start.1
  195.5 2.2 slice-start
  199.0 2.2 slice-start.1
  230.5 2.2 slice-start.1
  258.4 2.2 slice-start
  261.9 2.2 slice-start.1
  266.7 4.1 copy-start.2
  269.7 163.7 %all-gather.3.cloned.1.call-start = ((), (), s32[]{:S(2)}) async-start(), calls=%async_computation.2 | async-start | bytes 10948608 | tf_op jit(solution)/shard_map/all_gather | solution.py:115
  270.3 230.2 %all-gather.5.cloned.1.call-start = ((), (), s32[]{:S(2)}) async-start(), calls=%async_computation.3 | async-start | bytes 10948608 | tf_op jit(solution)/shard_map/all_gather | solution.py:119
  275.4 63.2 %copy-start.4 = (f32[2304]{0:T(1024)S(1)}, f32[2304]{0:T(1024)}, u32[]{:S(2)}) copy-start(f32[2304]{0:T(1024)} %param.24) | copy-start | bytes 27652
  275.4 237.9 %all-to-all-start = ((bf16[32,72,2304]{2,1,0:T(8,128)(2,1)}), bf16[32,72,2304]{2,1,0:T(8,128)(2,1)}, u32[]{:S(2)}, u32[]{:S(2)}) async-start(bf16[32,72,2304]{2,1,0:T(8,128)(2,1)} %stack.2), calls=%async_computation | async-start | bytes 21233664 | tf_op jit(solution)/shard_map/all_to_all | solution.py:125
  284.2 304.0 %all-reduce.5.cloned.1.call-start = ((), (), s32[]{:S(2)}) async-start(), calls=%async_computation.4 | async-start | bytes 4866048 | tf_op jit(solution)/shard_map/psum | solution.py:133
  338.6 94.8 %copy-start.5 = (f32[2304]{0:T(1024)S(1)}, f32[2304]{0:T(1024)}, u32[]{:S(2)}) copy-start(f32[2304]{0:T(1024)} %param.25) | copy-start | bytes 27652
  590.4 5.4 copy-start.1
  (10 other events, 9.7 us)
Sparse Core Ops, SparseCore 0:
  269.8 66.5 all-reduce.2
  525.0 63.1 all-reduce.4
Sparse Core Ops, SparseCore 1:
  272.5 160.8 all-gather.2
  435.6 64.8 all-gather.4
